TPU v7x, 512 devices: a whole 4x8x8 slice. The times are simulated.
512 devices in a mesh: group: 8 (over y), mesh: 32 (over z, x), comp: 2 (over core).
Axes of the slice: x: 4, y: 8, z: 8, core: 2. Of those that a mesh axis runs over, the one named last changes fastest.
Arguments:
- log_sigma: float32 [2048, 128], P('mesh'), may hold values from -1 to 1
- block_owner: int32 [8, 4096, 1], P('group', 'mesh'), may hold values from 0 to 31; in each aligned block of 128 rows (0 to 127, 128 to 255, ..., all dimensions but the last counted through in order) at most 8 rows name the same one
- block_slot: int32 [8, 4096], P('group', 'mesh'), may hold values from 0 to 63
- coupling: float32 [128, 128], replicated, may hold values from -0.6 to 10, as said below
- sources: float32 [8, 2, 8, 4096, 128], P('group', 'comp', None, 'mesh'), may hold values from -24 to 24
- rcv_cell: int32 [8, 4096], P('group', 'mesh'), may hold values from 0 to 16383
- observed: float32 [8, 2, 8, 4096], P('group', 'comp', None, 'mesh'), may hold values from -6 to 6
Outputs:
- gradient: float32 [2048, 128], P('mesh')
Inputs may be any that keep to these rules, and one draw needn't show every extreme that they name: `block_owner`: in the 128 rows of one device of a group, no owner is named more than 8 times; some owner is named exactly 8 times in some device's rows. `rcv_cell`: A receiver's cell counts from the first cell of the modelling section of the device that holds the receiver's entry. `coupling`: every diagonal entry is 6 or more.
All inputs are finite; a program needn't handle non-finite values.
Results may differ from a plain program's by a relative error of at most 0.0003.
Values sent between devices are 32-bit elements; how exact they have to be, the bound alone decides.
A program may use at most 64 MiB of HBM per device.

v0:
```python
import jax
import jax.numpy as jnp
from jax import lax
from jax.sharding import PartitionSpec as P

CELLS = 128
S = 8
ITERS = 6
omega_freq = 0.8
chain_weight = 1.0


def from_partner(value, axis, distance):
    mask = 2**distance
    pairs = [(source, source ^ mask) for source in range(lax.axis_size(axis))]
    return lax.ppermute(value, axis, pairs)


def with_halo(x, sides, width):
    for axis, dim in sides:
        size, length = (lax.axis_size(axis), x.shape[dim])
        up = [(i, (i + 1) % size) for i in range(size - 1)]
        down = [(j, i) for i, j in up]
        last = lax.slice_in_dim(x, length - width, length, axis=dim)
        initial = lax.slice_in_dim(x, 0, width, axis=dim)
        before = lax.ppermute(last, axis, up)
        after = lax.ppermute(initial, axis, down)
        x = jnp.concatenate([before, x, after], axis=dim)
    return x


def partner(values):
    return from_partner(values, "comp", 0)


def beside(values):
    padded = with_halo(values, (("mesh", 1),), 1)
    return padded[:, :-2] + padded[:, 2:]


def cell_product(values, matrix):
    shaped = values.reshape(values.shape[:-1] + (-1, CELLS))
    product = jnp.einsum("...bj,ij->...bi", shaped, matrix, precision=lax.Precision.HIGHEST)
    return product.reshape(values.shape)


def operate(values, matrix, cross_coef):
    return (
        cell_product(values, matrix) - chain_weight * beside(values) + cross_coef * partner(values)
    )


def relax(right, matrix, cross_coef, inverse_diag, apply_op):
    state = jnp.zeros_like(right)
    for iteration in range(ITERS):
        state = state + inverse_diag * (right - apply_op(state, matrix, cross_coef))
    return state


def local(log_sigma, block_owner, block_slot, coupling, sources, rcv_cell, observed):
    owners = block_owner[0, :, 0]
    slots = block_slot[0]
    blocks_dev = owners.shape[0]
    inv_rows = log_sigma.shape[0]
    targets = owners * inv_rows + slots
    gathered = lax.all_gather(log_sigma, "mesh", axis=0, tiled=True)
    model_part = jnp.take(gathered, targets, axis=0)
    sigmas = jnp.exp(model_part).reshape(-1)
    receivers = rcv_cell[0]
    parity = (2 * lax.axis_index("comp") - 1).astype(jnp.float32)
    forward_coef = parity * omega_freq * sigmas
    inverse_diag = jnp.tile(1.0 / jnp.diagonal(coupling), blocks_dev)
    right = sources.reshape(S, -1)
    field_now = relax(right, coupling, forward_coef, inverse_diag, operate)
    field_other = partner(field_now)
    misfit = field_now[:, receivers] - observed[0, 0]
    adjoint_src = jnp.zeros_like(right).at[:, receivers].add(misfit)
    adjoint = relax(adjoint_src, coupling.T, -forward_coef, inverse_diag, operate)
    weighted = -parity * jnp.sum(adjoint * field_other, axis=0)
    partial_rows = (omega_freq * sigmas * weighted).reshape(blocks_dev, CELLS)
    inside_rows = (targets >= 0) & (targets < inv_rows * lax.axis_size("mesh"))
    kept_rows = jnp.where(inside_rows, targets, inv_rows * lax.axis_size("mesh"))
    owned = lax.psum_scatter(
        jnp.zeros((inv_rows * lax.axis_size("mesh"), CELLS), jnp.float32)
        .at[kept_rows]
        .add(partial_rows, mode="drop"),
        "mesh",
        scatter_dimension=0,
        tiled=True,
    )
    return lax.psum(owned, ("group", "comp"))


def solution(mesh):
    in_specs = (
        P("mesh", None),
        P("group", "mesh", None),
        P("group", "mesh"),
        P(),
        P("group", "comp", None, "mesh", None),
        P("group", "mesh"),
        P("group", "comp", None, "mesh"),
    )
    out_specs = P("mesh", None)
    return jax.shard_map(local, mesh=mesh, in_specs=in_specs, out_specs=out_specs, check_vma=False)
```

profile of v0, /device:TPU:32, one launch (start us, length us, event | category | flops | bytes accessed | tf_op | source)
XLA Modules:
  0.0 532.8 jit_solution(2460921501740615536)
XLA Ops:
  6.5 0.7 all-gather.2.cloned.1.call-update
  7.3 1.3 collective-permute-start.1
  8.6 4.5 collective-permute-start
  13.2 1.9 collective-permute-start.2
  15.2 1.2 gather_fusion.1
  17.0 0.7 compare_and_fusion
  17.7 0.7 fusion.121
  18.4 78.7 %all-gather.2.cloned.1.call-done = f32[2048,128]{1,0:T(8,128)} async-done(((f32[64,128]{1,0:T(8,128)}), f32[2048,128]{1,0:T(8,128)}) %all-gather.2.cloned.1.call-update) | async-done | bytes 1048592 | tf_op jit(solution)/shard_map/all_gather | solution.py:66
  97.1 1.9 gather_fusion
  99.1 1.7 fusion.8
  100.8 1.9 collective-permute-start.5
  102.8 1.3 collective-permute-start.4
  104.1 4.5 collective-permute-start.3
  108.6 1.3 collective-permute-done.3
  109.9 1.9 fusion.10
  111.9 1.9 collective-permute-start.8
  113.9 1.3 collective-permute-start.7
  115.2 4.8 collective-permute-start.6
  120.0 0.6 convolution_bitcast_fusion.8
  120.6 0.7 collective-permute-done.6
  121.8 1.9 collective-permute-start.11
  123.8 1.3 collective-permute-start.10
  125.1 4.8 collective-permute-start.9
  129.9 1.3 collective-permute-done.9
  131.2 0.9 fusion.14
  132.1 1.9 collective-permute-start.14
  134.1 1.3 collective-permute-start.13
  135.4 4.8 collective-permute-start.12
  140.2 0.6 convolution_bitcast_fusion.6
  140.8 0.7 collective-permute-done.12
  142.1 1.9 collective-permute-start.17
  144.8 1.3 collective-permute-start.16
  146.1 5.5 %collective-permute-start.15 = (f32[8,1]{1,0:T(8,128)S(1)}, f32[8,1]{1,0:T(8,128)S(1)}, u32[]{:S(2)}, u32[]{:S(2)}) collective-permute-start(f32[8,1]{1,0:T(8,128)S(1)} %get-tuple-element.17), channel_id=1, source_target_pairs={{0,2},{2,4},{4,6},{6,8},{8,10},{10,12},{12,14},{14,16},{16,18},{18... | collective-permute-start | bytes 104 | tf_op jit(solution)/shard_map/ppermute | solution.py:26
  151.6 1.3 collective-permute-done.15
  152.9 1.9 fusion.18
  154.8 5.3 copy.271
  160.1 6.0 %scatter_custom_fusion = f32[8,16384]{0,1:T(8,128)} fusion(s32[128]{0:T(128)S(1)} %fusion.122, f32[]{:T(128)} %constant.12.clone.1, f32[1,1,8,128]{2,3,1,0:T(8,128)S(1)} %copy.272, f32[8,16384]{0,1:T(8,128)} %copy.271, s32[1024]{0:T(1024)S(1)} %pad_clamp_fusion), kind=kCustom, calls=%fused_computation.15 | custom fusion | flops 2048 | bytes 1118212 | tf_op jit(solution)/shard_map/scatter-add | solution.py:77
  166.1 5.5 %copy.273 = f32[8,16384]{1,0:T(8,128)S(1)} copy(f32[8,16384]{0,1:T(8,128)} %scatter_custom_fusion) | data formatting | bytes 1048576 | tf_op jit(solution)/shard_map/scatter-add | solution.py:77
  172.0 1.9 collective-permute-start.20
  174.0 1.3 collective-permute-start.19
  175.3 6.9 %collective-permute-start.18 = (f32[8,1]{1,0:T(8,128)S(1)}, f32[8,1]{1,0:T(8,128)S(1)}, u32[]{:S(2)}, u32[]{:S(2)}) collective-permute-start(f32[8,1]{1,0:T(8,128)S(1)} %get-tuple-element.15), channel_id=1, source_target_pairs={{0,2},{2,4},{4,6},{6,8},{8,10},{10,12},{12,14},{14,16},{16,18},{18... | collective-permute-start | bytes 104 | tf_op jit(solution)/shard_map/ppermute | solution.py:26
  182.3 1.3 collective-permute-done.18
  183.6 0.7 fusion.50
  184.2 1.9 collective-permute-start.23
  186.2 1.3 collective-permute-start.22
  187.5 6.9 %collective-permute-start.21 = (f32[8,1]{1,0:T(8,128)S(1)}, f32[8,1]{1,0:T(8,128)S(1)}, u32[]{:S(2)}, u32[]{:S(2)}) collective-permute-start(f32[8,1]{1,0:T(8,128)S(1)} %get-tuple-element.13), channel_id=1, source_target_pairs={{0,2},{2,4},{4,6},{6,8},{8,10},{10,12},{12,14},{14,16},{16,18},{18... | collective-permute-start | bytes 104 | tf_op jit(solution)/shard_map/ppermute | solution.py:26
  195.0 0.7 collective-permute-done.21
  196.2 1.9 collective-permute-start.26
  198.2 1.3 collective-permute-start.25
  199.5 6.9 %collective-permute-start.24 = (f32[8,1]{1,0:T(8,128)S(1)}, f32[8,1]{1,0:T(8,128)S(1)}, u32[]{:S(2)}, u32[]{:S(2)}) collective-permute-start(f32[8,1]{1,0:T(8,128)S(1)} %get-tuple-element.11), channel_id=1, source_target_pairs={{0,2},{2,4},{4,6},{6,8},{8,10},{10,12},{12,14},{14,16},{16,18},{18... | collective-permute-start | bytes 104 | tf_op jit(solution)/shard_map/ppermute | solution.py:26
  206.4 1.3 collective-permute-done.24
  207.7 0.7 fusion.38
  208.4 1.9 collective-permute-start.29
  210.3 2.4 collective-permute-start.33
  212.8 1.3 collective-permute-start.28
  214.1 6.9 %collective-permute-start.27 = (f32[8,1]{1,0:T(8,128)S(1)}, f32[8,1]{1,0:T(8,128)S(1)}, u32[]{:S(2)}, u32[]{:S(2)}) collective-permute-start(f32[8,1]{1,0:T(8,128)S(1)} %get-tuple-element.9), channel_id=1, source_target_pairs={{0,2},{2,4},{4,6},{6,8},{8,10},{10,12},{12,14},{14,16},{16,18},{18... | collective-permute-start | bytes 104 | tf_op jit(solution)/shard_map/ppermute | solution.py:26
  221.6 0.7 collective-permute-done.27
  222.8 1.9 collective-permute-start.32
  224.8 1.3 collective-permute-start.31
  226.1 6.9 %collective-permute-start.30 = (f32[8,1]{1,0:T(8,128)S(1)}, f32[8,1]{1,0:T(8,128)S(1)}, u32[]{:S(2)}, u32[]{:S(2)}) collective-permute-start(f32[8,1]{1,0:T(8,128)S(1)} %get-tuple-element.7), channel_id=1, source_target_pairs={{0,2},{2,4},{4,6},{6,8},{8,10},{10,12},{12,14},{14,16},{16,18},{18... | collective-permute-start | bytes 104 | tf_op jit(solution)/shard_map/ppermute | solution.py:26
  233.6 0.7 collective-permute-done.30
  234.7 2.1 scatter_custom_fusion.1
  236.8 242.3 %reduce-scatter.2.cloned.1.call-done = f32[64,128]{1,0:T(8,128)} async-done(((f32[2048,128]{1,0:T(8,128)}), f32[64,128]{1,0:T(8,128)}) %reduce-scatter.2.cloned.1.call-update) | async-done | bytes 32784 | tf_op jit(solution)/shard_map/reduce_scatter | solution.py:83
  479.1 46.9 %psum.7 = f32[64,128]{1,0:T(8,128)} all-reduce(f32[64,128]{1,0:T(8,128)} %reduce-scatter.2.cloned.1.call-done), channel_id=1, replica_groups=mesh['group'=8,'mesh'=32,'comp'=2] {'group','comp'}, use_global_device_ids=true, to_apply=%region_4.5 | all-reduce | flops 8192 | bytes 65536 | tf_op jit(solution)/shard_map/psum | solution.py:91
  (66 shorter events, 6.6 us)
Async XLA Ops:
  6.5 8.7 %copy-start = (f32[128,128]{1,0:T(8,128)S(1)}, f32[128,128]{1,0:T(8,128)}, u32[]{:S(2)}) copy-start(f32[128,128]{1,0:T(8,128)} %param.10) | copy-start | bytes 196612
  6.5 114.8 %copy-start.1 = (f32[1,1,8,128,128]{4,3,2,1,0:T(8,128)S(1)}, f32[1,1,8,128,128]{4,3,2,1,0:T(8,128)}, u32[]{:S(2)}) copy-start(f32[1,1,8,128,128]{4,3,2,1,0:T(8,128)} %param.11) | copy-start | bytes 1572868
  6.5 90.6 %all-gather.2.cloned.1.call-start = ((), (), s32[]{:S(2)}) async-start(), calls=%async_computation.1 | async-start | bytes 1081344 | tf_op jit(solution)/shard_map/all_gather | solution.py:66
  7.3 471.8 %reduce-scatter.2.cloned.1.call-start = ((), (), s32[]{:S(2)}) async-start(), calls=%async_computation.2 | async-start | bytes 1081344 | tf_op jit(solution)/shard_map/reduce_scatter | solution.py:83
  7.3 91.8 %collective-permute-start.1 = (f32[8,1]{1,0:T(8,128)S(1)}, f32[8,1]{1,0:T(8,128)S(1)}, u32[]{:S(2)}, u32[]{:S(2)}) collective-permute-start(f32[8,1]{1,0:T(8,128)S(1)} %broadcast.157), channel_id=1, source_target_pairs={{2,0},{4,2},{6,4},{8,6},{10,8},{12,10},{14,12},{16,14},{18,16},{20... | collective-permute-start | bytes 104 | tf_op jit(solution)/shard_map/ppermute | solution.py:27
  8.6 90.5 %collective-permute-start = (f32[8,1]{1,0:T(8,128)S(1)}, f32[8,1]{1,0:T(8,128)S(1)}, u32[]{:S(2)}, u32[]{:S(2)}) collective-permute-start(f32[8,1]{1,0:T(8,128)S(1)} %broadcast.157), channel_id=1, source_target_pairs={{0,2},{2,4},{4,6},{6,8},{8,10},{10,12},{12,14},{14,16},{16,18},{18... | collective-permute-start | bytes 104 | tf_op jit(solution)/shard_map/ppermute | solution.py:26
  13.2 130.8 %copy-start.3 = (s32[1,128]{1,0:T(1,128)S(1)}, s32[1,128]{1,0:T(1,128)}, u32[]{:S(2)}) copy-start(s32[1,128]{1,0:T(1,128)} %param.12) | copy-start | bytes 1540
  13.2 130.8 %copy-start.2 = (f32[1,1,8,128]{3,2,1,0:T(8,128)S(1)}, f32[1,1,8,128]{3,2,1,0:T(8,128)}, u32[]{:S(2)}) copy-start(f32[1,1,8,128]{3,2,1,0:T(8,128)} %param.13) | copy-start | bytes 12292
  13.2 85.8 %collective-permute-start.2 = (f32[8,16384]{1,0:T(8,128)S(1)}, f32[8,16384]{1,0:T(8,128)S(1)}, u32[]{:S(2)}, u32[]{:S(2)}) collective-permute-start(f32[8,16384]{1,0:T(8,128)S(1)} %broadcast.154.clone), channel_id=1, source_target_pairs={{0,1},{1,0},{2,3},{3,2},{4,5},{5,4},{6,7},{7,6},{8,9},{9,8},{10,11... | collective-permute-start | bytes 1572872 | tf_op jit(solution)/shard_map/ppermute | solution.py:16
  100.8 9.2 %collective-permute-start.5 = (f32[8,16384]{1,0:T(8,128)S(1)}, f32[8,16384]{1,0:T(8,128)S(1)}, u32[]{:S(2)}, u32[]{:S(2)}) collective-permute-start(f32[8,16384]{1,0:T(8,128)S(1)} %fusion.8), channel_id=1, source_target_pairs={{0,1},{1,0},{2,3},{3,2},{4,5},{5,4},{6,7},{7,6},{8,9},{9,8},{10,11... | collective-permute-start | bytes 1572872 | tf_op jit(solution)/shard_map/ppermute | solution.py:16
  102.8 5.8 %collective-permute-start.4 = (f32[8,1]{1,0:T(8,128)S(1)}, f32[8,1]{1,0:T(8,128)S(1)}, u32[]{:S(2)}, u32[]{:S(2)}) collective-permute-start(f32[8,1]{1,0:T(8,128)S(1)} %get-tuple-element.26), channel_id=1, source_target_pairs={{2,0},{4,2},{6,4},{8,6},{10,8},{12,10},{14,12},{16,14},{18,16},{20... | collective-permute-start | bytes 104 | tf_op jit(solution)/shard_map/ppermute | solution.py:27
  104.1 5.9 %collective-permute-start.3 = (f32[8,1]{1,0:T(8,128)S(1)}, f32[8,1]{1,0:T(8,128)S(1)}, u32[]{:S(2)}, u32[]{:S(2)}) collective-permute-start(f32[8,1]{1,0:T(8,128)S(1)} %get-tuple-element.25), channel_id=1, source_target_pairs={{0,2},{2,4},{4,6},{6,8},{8,10},{10,12},{12,14},{14,16},{16,18},{18... | collective-permute-start | bytes 104 | tf_op jit(solution)/shard_map/ppermute | solution.py:26
  111.9 9.4 %collective-permute-start.8 = (f32[8,16384]{1,0:T(8,128)S(1)}, f32[8,16384]{1,0:T(8,128)S(1)}, u32[]{:S(2)}, u32[]{:S(2)}) collective-permute-start(f32[8,16384]{1,0:T(8,128)S(1)} %fusion.10), channel_id=1, source_target_pairs={{0,1},{1,0},{2,3},{3,2},{4,5},{5,4},{6,7},{7,6},{8,9},{9,8},{10,11... | collective-permute-start | bytes 1572872 | tf_op jit(solution)/shard_map/ppermute | solution.py:16
  113.9 6.7 %collective-permute-start.7 = (f32[8,1]{1,0:T(8,128)S(1)}, f32[8,1]{1,0:T(8,128)S(1)}, u32[]{:S(2)}, u32[]{:S(2)}) collective-permute-start(f32[8,1]{1,0:T(8,128)S(1)} %get-tuple-element.24), channel_id=1, source_target_pairs={{2,0},{4,2},{6,4},{8,6},{10,8},{12,10},{14,12},{16,14},{18,16},{20... | collective-permute-start | bytes 104 | tf_op jit(solution)/shard_map/ppermute | solution.py:27
  115.2 6.1 %collective-permute-start.6 = (f32[8,1]{1,0:T(8,128)S(1)}, f32[8,1]{1,0:T(8,128)S(1)}, u32[]{:S(2)}, u32[]{:S(2)}) collective-permute-start(f32[8,1]{1,0:T(8,128)S(1)} %get-tuple-element.23), channel_id=1, source_target_pairs={{0,2},{2,4},{4,6},{6,8},{8,10},{10,12},{12,14},{14,16},{16,18},{18... | collective-permute-start | bytes 104 | tf_op jit(solution)/shard_map/ppermute | solution.py:26
  121.8 9.4 %collective-permute-start.11 = (f32[8,16384]{1,0:T(8,128)S(1)}, f32[8,16384]{1,0:T(8,128)S(1)}, u32[]{:S(2)}, u32[]{:S(2)}) collective-permute-start(f32[8,16384]{1,0:T(8,128)S(1)} %fusion.12), channel_id=1, source_target_pairs={{0,1},{1,0},{2,3},{3,2},{4,5},{5,4},{6,7},{7,6},{8,9},{9,8},{10,11... | collective-permute-start | bytes 1572872 | tf_op jit(solution)/shard_map/ppermute | solution.py:16
  123.8 6.1 %collective-permute-start.10 = (f32[8,1]{1,0:T(8,128)S(1)}, f32[8,1]{1,0:T(8,128)S(1)}, u32[]{:S(2)}, u32[]{:S(2)}) collective-permute-start(f32[8,1]{1,0:T(8,128)S(1)} %get-tuple-element.22), channel_id=1, source_target_pairs={{2,0},{4,2},{6,4},{8,6},{10,8},{12,10},{14,12},{16,14},{18,16},{20... | collective-permute-start | bytes 104 | tf_op jit(solution)/shard_map/ppermute | solution.py:27
  125.1 6.1 %collective-permute-start.9 = (f32[8,1]{1,0:T(8,128)S(1)}, f32[8,1]{1,0:T(8,128)S(1)}, u32[]{:S(2)}, u32[]{:S(2)}) collective-permute-start(f32[8,1]{1,0:T(8,128)S(1)} %get-tuple-element.21), channel_id=1, source_target_pairs={{0,2},{2,4},{4,6},{6,8},{8,10},{10,12},{12,14},{14,16},{16,18},{18... | collective-permute-start | bytes 104 | tf_op jit(solution)/shard_map/ppermute | solution.py:26
  132.1 9.4 %collective-permute-start.14 = (f32[8,16384]{1,0:T(8,128)S(1)}, f32[8,16384]{1,0:T(8,128)S(1)}, u32[]{:S(2)}, u32[]{:S(2)}) collective-permute-start(f32[8,16384]{1,0:T(8,128)S(1)} %fusion.14), channel_id=1, source_target_pairs={{0,1},{1,0},{2,3},{3,2},{4,5},{5,4},{6,7},{7,6},{8,9},{9,8},{10,11... | collective-permute-start | bytes 1572872 | tf_op jit(solution)/shard_map/ppermute | solution.py:16
  134.1 6.7 %collective-permute-start.13 = (f32[8,1]{1,0:T(8,128)S(1)}, f32[8,1]{1,0:T(8,128)S(1)}, u32[]{:S(2)}, u32[]{:S(2)}) collective-permute-start(f32[8,1]{1,0:T(8,128)S(1)} %get-tuple-element.20), channel_id=1, source_target_pairs={{2,0},{4,2},{6,4},{8,6},{10,8},{12,10},{14,12},{16,14},{18,16},{20... | collective-permute-start | bytes 104 | tf_op jit(solution)/shard_map/ppermute | solution.py:27
  135.4 6.1 %collective-permute-start.12 = (f32[8,1]{1,0:T(8,128)S(1)}, f32[8,1]{1,0:T(8,128)S(1)}, u32[]{:S(2)}, u32[]{:S(2)}) collective-permute-start(f32[8,1]{1,0:T(8,128)S(1)} %get-tuple-element.19), channel_id=1, source_target_pairs={{0,2},{2,4},{4,6},{6,8},{8,10},{10,12},{12,14},{14,16},{16,18},{18... | collective-permute-start | bytes 104 | tf_op jit(solution)/shard_map/ppermute | solution.py:26
  142.1 10.8 %collective-permute-start.17 = (f32[8,16384]{1,0:T(8,128)S(1)}, f32[8,16384]{1,0:T(8,128)}, u32[]{:S(2)}, u32[]{:S(2)}) collective-permute-start(f32[8,16384]{1,0:T(8,128)S(1)} %fusion.16), channel_id=1, source_target_pairs={{0,1},{1,0},{2,3},{3,2},{4,5},{5,4},{6,7},{7,6},{8,9},{9,8},{10,11... | collective-permute-start | bytes 1572872 | tf_op jit(solution)/shard_map/ppermute | solution.py:16
  144.8 6.8 %collective-permute-start.16 = (f32[8,1]{1,0:T(8,128)S(1)}, f32[8,1]{1,0:T(8,128)S(1)}, u32[]{:S(2)}, u32[]{:S(2)}) collective-permute-start(f32[8,1]{1,0:T(8,128)S(1)} %get-tuple-element.18), channel_id=1, source_target_pairs={{2,0},{4,2},{6,4},{8,6},{10,8},{12,10},{14,12},{16,14},{18,16},{20... | collective-permute-start | bytes 104 | tf_op jit(solution)/shard_map/ppermute | solution.py:27
  146.1 6.8 %collective-permute-start.15 = (f32[8,1]{1,0:T(8,128)S(1)}, f32[8,1]{1,0:T(8,128)S(1)}, u32[]{:S(2)}, u32[]{:S(2)}) collective-permute-start(f32[8,1]{1,0:T(8,128)S(1)} %get-tuple-element.17), channel_id=1, source_target_pairs={{0,2},{2,4},{4,6},{6,8},{8,10},{10,12},{12,14},{14,16},{16,18},{18... | collective-permute-start | bytes 104 | tf_op jit(solution)/shard_map/ppermute | solution.py:26
  172.0 11.5 %collective-permute-start.20 = (f32[8,16384]{1,0:T(8,128)S(1)}, f32[8,16384]{1,0:T(8,128)S(1)}, u32[]{:S(2)}, u32[]{:S(2)}) collective-permute-start(f32[8,16384]{1,0:T(8,128)S(1)} %fusion.5), channel_id=1, source_target_pairs={{0,1},{1,0},{2,3},{3,2},{4,5},{5,4},{6,7},{7,6},{8,9},{9,8},{10,11... | collective-permute-start | bytes 1572872 | tf_op jit(solution)/shard_map/ppermute | solution.py:16
  174.0 8.2 %collective-permute-start.19 = (f32[8,1]{1,0:T(8,128)S(1)}, f32[8,1]{1,0:T(8,128)S(1)}, u32[]{:S(2)}, u32[]{:S(2)}) collective-permute-start(f32[8,1]{1,0:T(8,128)S(1)} %get-tuple-element.16), channel_id=1, source_target_pairs={{2,0},{4,2},{6,4},{8,6},{10,8},{12,10},{14,12},{16,14},{18,16},{20... | collective-permute-start | bytes 104 | tf_op jit(solution)/shard_map/ppermute | solution.py:27
  175.3 8.3 %collective-permute-start.18 = (f32[8,1]{1,0:T(8,128)S(1)}, f32[8,1]{1,0:T(8,128)S(1)}, u32[]{:S(2)}, u32[]{:S(2)}) collective-permute-start(f32[8,1]{1,0:T(8,128)S(1)} %get-tuple-element.15), channel_id=1, source_target_pairs={{0,2},{2,4},{4,6},{6,8},{8,10},{10,12},{12,14},{14,16},{16,18},{18... | collective-permute-start | bytes 104 | tf_op jit(solution)/shard_map/ppermute | solution.py:26
  184.2 11.5 %collective-permute-start.23 = (f32[8,16384]{1,0:T(8,128)S(1)}, f32[8,16384]{1,0:T(8,128)S(1)}, u32[]{:S(2)}, u32[]{:S(2)}) collective-permute-start(f32[8,16384]{1,0:T(8,128)S(1)} %fusion.50), channel_id=1, source_target_pairs={{0,1},{1,0},{2,3},{3,2},{4,5},{5,4},{6,7},{7,6},{8,9},{9,8},{10,11... | collective-permute-start | bytes 1572872 | tf_op jit(solution)/shard_map/ppermute | solution.py:16
  186.2 8.8 %collective-permute-start.22 = (f32[8,1]{1,0:T(8,128)S(1)}, f32[8,1]{1,0:T(8,128)S(1)}, u32[]{:S(2)}, u32[]{:S(2)}) collective-permute-start(f32[8,1]{1,0:T(8,128)S(1)} %get-tuple-element.14), channel_id=1, source_target_pairs={{2,0},{4,2},{6,4},{8,6},{10,8},{12,10},{14,12},{16,14},{18,16},{20... | collective-permute-start | bytes 104 | tf_op jit(solution)/shard_map/ppermute | solution.py:27
  187.5 8.2 %collective-permute-start.21 = (f32[8,1]{1,0:T(8,128)S(1)}, f32[8,1]{1,0:T(8,128)S(1)}, u32[]{:S(2)}, u32[]{:S(2)}) collective-permute-start(f32[8,1]{1,0:T(8,128)S(1)} %get-tuple-element.13), channel_id=1, source_target_pairs={{0,2},{2,4},{4,6},{6,8},{8,10},{10,12},{12,14},{14,16},{16,18},{18... | collective-permute-start | bytes 104 | tf_op jit(solution)/shard_map/ppermute | solution.py:26
  196.2 11.5 %collective-permute-start.26 = (f32[8,16384]{1,0:T(8,128)S(1)}, f32[8,16384]{1,0:T(8,128)S(1)}, u32[]{:S(2)}, u32[]{:S(2)}) collective-permute-start(f32[8,16384]{1,0:T(8,128)S(1)} %fusion.44), channel_id=1, source_target_pairs={{0,1},{1,0},{2,3},{3,2},{4,5},{5,4},{6,7},{7,6},{8,9},{9,8},{10,11... | collective-permute-start | bytes 1572872 | tf_op jit(solution)/shard_map/ppermute | solution.py:16
  198.2 8.2 %collective-permute-start.25 = (f32[8,1]{1,0:T(8,128)S(1)}, f32[8,1]{1,0:T(8,128)S(1)}, u32[]{:S(2)}, u32[]{:S(2)}) collective-permute-start(f32[8,1]{1,0:T(8,128)S(1)} %get-tuple-element.12), channel_id=1, source_target_pairs={{2,0},{4,2},{6,4},{8,6},{10,8},{12,10},{14,12},{16,14},{18,16},{20... | collective-permute-start | bytes 104 | tf_op jit(solution)/shard_map/ppermute | solution.py:27
  199.5 8.2 %collective-permute-start.24 = (f32[8,1]{1,0:T(8,128)S(1)}, f32[8,1]{1,0:T(8,128)S(1)}, u32[]{:S(2)}, u32[]{:S(2)}) collective-permute-start(f32[8,1]{1,0:T(8,128)S(1)} %get-tuple-element.11), channel_id=1, source_target_pairs={{0,2},{2,4},{4,6},{6,8},{8,10},{10,12},{12,14},{14,16},{16,18},{18... | collective-permute-start | bytes 104 | tf_op jit(solution)/shard_map/ppermute | solution.py:26
  208.4 14.0 %collective-permute-start.29 = (f32[8,16384]{1,0:T(8,128)S(1)}, f32[8,16384]{1,0:T(8,128)S(1)}, u32[]{:S(2)}, u32[]{:S(2)}) collective-permute-start(f32[8,16384]{1,0:T(8,128)S(1)} %fusion.38), channel_id=1, source_target_pairs={{0,1},{1,0},{2,3},{3,2},{4,5},{5,4},{6,7},{7,6},{8,9},{9,8},{10,11... | collective-permute-start | bytes 1572872 | tf_op jit(solution)/shard_map/ppermute | solution.py:16
  210.3 23.2 %collective-permute-start.33 = (f32[8,16384]{1,0:T(8,128)S(1)}, f32[8,16384]{1,0:T(8,128)S(1)}, u32[]{:S(2)}, u32[]{:S(2)}) collective-permute-start(f32[8,16384]{1,0:T(8,128)S(1)} %fusion.18), channel_id=1, source_target_pairs={{0,1},{1,0},{2,3},{3,2},{4,5},{5,4},{6,7},{7,6},{8,9},{9,8},{10,11... | collective-permute-start | bytes 1572872 | tf_op jit(solution)/shard_map/ppermute | solution.py:16
  212.8 8.8 %collective-permute-start.28 = (f32[8,1]{1,0:T(8,128)S(1)}, f32[8,1]{1,0:T(8,128)S(1)}, u32[]{:S(2)}, u32[]{:S(2)}) collective-permute-start(f32[8,1]{1,0:T(8,128)S(1)} %get-tuple-element.10), channel_id=1, source_target_pairs={{2,0},{4,2},{6,4},{8,6},{10,8},{12,10},{14,12},{16,14},{18,16},{20... | collective-permute-start | bytes 104 | tf_op jit(solution)/shard_map/ppermute | solution.py:27
  214.1 8.3 %collective-permute-start.27 = (f32[8,1]{1,0:T(8,128)S(1)}, f32[8,1]{1,0:T(8,128)S(1)}, u32[]{:S(2)}, u32[]{:S(2)}) collective-permute-start(f32[8,1]{1,0:T(8,128)S(1)} %get-tuple-element.9), channel_id=1, source_target_pairs={{0,2},{2,4},{4,6},{6,8},{8,10},{10,12},{12,14},{14,16},{16,18},{18... | collective-permute-start | bytes 104 | tf_op jit(solution)/shard_map/ppermute | solution.py:26
  222.8 11.5 %collective-permute-start.32 = (f32[8,16384]{1,0:T(8,128)S(1)}, f32[8,16384]{1,0:T(8,128)S(1)}, u32[]{:S(2)}, u32[]{:S(2)}) collective-permute-start(f32[8,16384]{1,0:T(8,128)S(1)} %fusion.32), channel_id=1, source_target_pairs={{0,1},{1,0},{2,3},{3,2},{4,5},{5,4},{6,7},{7,6},{8,9},{9,8},{10,11... | collective-permute-start | bytes 1572872 | tf_op jit(solution)/shard_map/ppermute | solution.py:16
  224.8 8.8 %collective-permute-start.31 = (f32[8,1]{1,0:T(8,128)S(1)}, f32[8,1]{1,0:T(8,128)S(1)}, u32[]{:S(2)}, u32[]{:S(2)}) collective-permute-start(f32[8,1]{1,0:T(8,128)S(1)} %get-tuple-element.8), channel_id=1, source_target_pairs={{2,0},{4,2},{6,4},{8,6},{10,8},{12,10},{14,12},{16,14},{18,16},{20... | collective-permute-start | bytes 104 | tf_op jit(solution)/shard_map/ppermute | solution.py:27
  226.1 8.2 %collective-permute-start.30 = (f32[8,1]{1,0:T(8,128)S(1)}, f32[8,1]{1,0:T(8,128)S(1)}, u32[]{:S(2)}, u32[]{:S(2)}) collective-permute-start(f32[8,1]{1,0:T(8,128)S(1)} %get-tuple-element.7), channel_id=1, source_target_pairs={{0,2},{2,4},{4,6},{6,8},{8,10},{10,12},{12,14},{14,16},{16,18},{18... | collective-permute-start | bytes 104 | tf_op jit(solution)/shard_map/ppermute | solution.py:26
Sparse Core Ops, SparseCore 0:
  10.5 86.5 all-gather.1
  237.0 242.0 reduce-scatter.1
where the time goes:
time: 534 us; the launch traced here: 533 us
  waiting for transfers between devices  332 us (62%)
  starting transfers between devices  101 us (19%)
  blocking collectives  46.9 us (9%)
  local copies, waits for them, and re-layouts  14.9 us (3%)
  between operations  14 us (3%)
  other arithmetic  13.9 us (3%)
  matrix products  10.1 us (2%)
    reduce_scatter x1, waiting for transfers between devices, local(): lax.psum_scatter(jnp.zeros((inv_rows * lax.axis_size('mesh'), CELLS), jnp...  242 us
    all_gather x1, waiting for transfers between devices, local(): gathered = lax.all_gather(log_sigma, 'mesh', axis=0, tiled=True)  78.7 us
    ppermute x11, starting transfers between devices, with_halo(): before = lax.ppermute(last, axis, up)  63.6 us
    psum x1, blocking collectives, local(): return lax.psum(owned, ('group', 'comp'))  46.9 us
    ppermute x12, starting transfers between devices, from_partner(): return lax.ppermute(value, axis, pairs)  23.5 us
    ppermute x11, starting transfers between devices, with_halo(): after = lax.ppermute(initial, axis, down)  14.1 us
  transfers between devices with their start and end apart: 36, of which 12 were waited for; matrix products, arithmetic and copies ran while one was open for 2% of the time, Pallas kernels for 0%

commit v1 on v0

--- a/solution.py
+++ b/solution.py
@@ -2,6 +2,7 @@
 import jax.numpy as jnp
 from jax import lax
 from jax.sharding import PartitionSpec as P
+from jax.lax import all_to_all, axis_size
 
 CELLS = 128
 S = 8
@@ -63,7 +64,9 @@
     blocks_dev = owners.shape[0]
     inv_rows = log_sigma.shape[0]
     targets = owners * inv_rows + slots
-    gathered = lax.all_gather(log_sigma, "mesh", axis=0, tiled=True)
+    side_arr = jnp.stack([log_sigma] * axis_size("mesh"))
+    b_next = all_to_all(side_arr, axis_name="mesh", split_axis=0, concat_axis=0)
+    gathered = jnp.concatenate(b_next, axis=0)
     model_part = jnp.take(gathered, targets, axis=0)
     sigmas = jnp.exp(model_part).reshape(-1)
     receivers = rcv_cell[0]

time: 534 us -> 484 us (0.906)
  waiting for transfers between devices: 332 us -> 267 us
  starting transfers between devices: 101 us -> 116 us
    all_gather x1 -> x0, waiting for transfers between devices: 78.7 us -> none  [local(): gathered = lax.all_gather(log_sigma, 'mesh', axis=0, tiled=True)]
    all_to_all x0 -> x1, waiting for transfers between devices: none -> 16.9 us  [local(): b_next = all_to_all(side_arr, axis_name='mesh', split_axis=0, concat_axis=0)]
    all_to_all x0 -> x1, starting transfers between devices: none -> 13.2 us  [local(): b_next = all_to_all(side_arr, axis_name='mesh', split_axis=0, concat_axis=0)]
where the time goes in v1:
time: 484 us; the launch traced here: 482 us
  waiting for transfers between devices  267 us (55%)
  starting transfers between devices  116 us (24%)
  blocking collectives  46.9 us (10%)
  local copies, waits for them, and re-layouts  15.5 us (3%)
  between operations  14 us (3%)
  other arithmetic  13.9 us (3%)
  matrix products  9.05 us (2%)
    reduce_scatter x1, waiting for transfers between devices, local(): lax.psum_scatter(jnp.zeros((inv_rows * lax.axis_size('mesh'), CELLS), jnp...  240 us
    ppermute x11, starting transfers between devices, with_halo(): before = lax.ppermute(last, axis, up)  64.8 us
    psum x1, blocking collectives, local(): return lax.psum(owned, ('group', 'comp'))  46.9 us
    ppermute x12, starting transfers between devices, from_partner(): return lax.ppermute(value, axis, pairs)  23.5 us
    all_to_all x1, waiting for transfers between devices, local(): b_next = all_to_all(side_arr, axis_name='mesh', split_axis=0, concat_axis=0)  16.9 us
    ppermute x11, starting transfers between devices, with_halo(): after = lax.ppermute(initial, axis, down)  14.1 us
    all_to_all x1, starting transfers between devices, local(): b_next = all_to_all(side_arr, axis_name='mesh', split_axis=0, concat_axis=0)  13.2 us
    ppermute x11, waiting for transfers between devices, with_halo(): before = lax.ppermute(last, axis, up)  10.1 us
  transfers between devices with their start and end apart: 36, of which 12 were waited for; matrix products, arithmetic and copies ran while one was open for 2% of the time, Pallas kernels for 0%

profile of v1, /device:TPU:32, one launch (start us, length us, event | category | flops | bytes accessed | tf_op | source)
XLA Modules:
  0.0 482.2 jit_solution(8464868465338218760)
XLA Ops:
  6.5 1.9 stack.2
  8.5 13.2 %all-to-all-start = ((f32[32,64,128]{2,1,0:T(8,128)}), f32[32,64,128]{2,1,0:T(8,128)S(1)}, u32[]{:S(2)}, u32[]{:S(2)}) async-start(f32[32,64,128]{2,1,0:T(8,128)} %stack.2), calls=%async_computation | async-start | bytes 2097152 | tf_op jit(solution)/shard_map/all_to_all | solution.py:68
  21.7 1.3 collective-permute-start.1
  23.0 4.5 collective-permute-start
  27.6 1.9 collective-permute-start.2
  29.6 1.2 gather_fusion.1
  31.4 0.7 compare_and_fusion
  32.1 0.7 fusion.121
  32.8 16.9 %all-to-all-done = f32[32,64,128]{2,1,0:T(8,128)S(1)} async-done(((f32[32,64,128]{2,1,0:T(8,128)}), f32[32,64,128]{2,1,0:T(8,128)S(1)}, u32[]{:S(2)}, u32[]{:S(2)}) %all-to-all-start) | async-done | bytes 1048608 | tf_op jit(solution)/shard_map/all_to_all | solution.py:68
  49.7 0.6 gather_fusion
  50.5 1.7 fusion.8
  52.1 1.9 collective-permute-start.5
  54.1 1.3 collective-permute-start.4
  55.4 4.5 collective-permute-start.3
  60.0 1.3 collective-permute-done.3
  61.3 0.9 fusion.10
  62.2 1.9 collective-permute-start.8
  64.2 1.3 collective-permute-start.7
  65.5 4.8 collective-permute-start.6
  70.3 0.6 convolution_bitcast_fusion.8
  70.9 0.7 collective-permute-done.6
  72.1 1.9 collective-permute-start.11
  74.1 1.3 collective-permute-start.10
  75.4 4.8 collective-permute-start.9
  80.2 1.3 collective-permute-done.9
  81.5 0.9 fusion.14
  82.5 1.9 collective-permute-start.14
  84.5 1.3 collective-permute-start.13
  85.7 4.8 collective-permute-start.12
  91.2 0.7 collective-permute-done.12
  92.4 1.9 collective-permute-start.17
  95.1 1.3 collective-permute-start.16
  96.4 6.7 %collective-permute-start.15 = (f32[8,1]{1,0:T(8,128)S(1)}, f32[8,1]{1,0:T(8,128)S(1)}, u32[]{:S(2)}, u32[]{:S(2)}) collective-permute-start(f32[8,1]{1,0:T(8,128)S(1)} %get-tuple-element.17), channel_id=1, source_target_pairs={{0,2},{2,4},{4,6},{6,8},{8,10},{10,12},{12,14},{14,16},{16,18},{18... | collective-permute-start | bytes 104 | tf_op jit(solution)/shard_map/ppermute | solution.py:27
  103.1 1.3 collective-permute-done.15
  104.4 1.9 fusion.18
  106.3 5.3 %copy.271 = f32[8,16384]{0,1:T(8,128)} copy(f32[8,16384]{1,0:T(8,128)S(1)} %fusion.18) | data formatting | bytes 1048576 | tf_op jit(solution)/shard_map/add | solution.py:57
  111.6 6.0 %scatter_custom_fusion = f32[8,16384]{0,1:T(8,128)} fusion(s32[128]{0:T(128)S(1)} %fusion.122, f32[]{:T(128)} %constant.12.clone.1, f32[1,1,8,128]{2,3,1,0:T(8,128)S(1)} %copy.272, f32[8,16384]{0,1:T(8,128)} %copy.271, s32[1024]{0:T(1024)S(1)} %pad_clamp_fusion), kind=kCustom, calls=%fused_computation.15 | custom fusion | flops 2048 | bytes 1118212 | tf_op jit(solution)/shard_map/scatter-add | solution.py:80
  117.6 5.5 %copy.273 = f32[8,16384]{1,0:T(8,128)S(1)} copy(f32[8,16384]{0,1:T(8,128)} %scatter_custom_fusion) | data formatting | bytes 1048576 | tf_op jit(solution)/shard_map/scatter-add | solution.py:80
  123.6 1.9 collective-permute-start.20
  125.6 1.3 collective-permute-start.19
  126.8 6.9 %collective-permute-start.18 = (f32[8,1]{1,0:T(8,128)S(1)}, f32[8,1]{1,0:T(8,128)S(1)}, u32[]{:S(2)}, u32[]{:S(2)}) collective-permute-start(f32[8,1]{1,0:T(8,128)S(1)} %get-tuple-element.15), channel_id=1, source_target_pairs={{0,2},{2,4},{4,6},{6,8},{8,10},{10,12},{12,14},{14,16},{16,18},{18... | collective-permute-start | bytes 104 | tf_op jit(solution)/shard_map/ppermute | solution.py:27
  133.8 1.3 collective-permute-done.18
  135.1 0.7 fusion.50
  135.7 1.9 collective-permute-start.23
  137.7 1.3 collective-permute-start.22
  139.0 6.9 %collective-permute-start.21 = (f32[8,1]{1,0:T(8,128)S(1)}, f32[8,1]{1,0:T(8,128)S(1)}, u32[]{:S(2)}, u32[]{:S(2)}) collective-permute-start(f32[8,1]{1,0:T(8,128)S(1)} %get-tuple-element.13), channel_id=1, source_target_pairs={{0,2},{2,4},{4,6},{6,8},{8,10},{10,12},{12,14},{14,16},{16,18},{18... | collective-permute-start | bytes 104 | tf_op jit(solution)/shard_map/ppermute | solution.py:27
  146.6 0.7 collective-permute-done.21
  147.7 1.9 collective-permute-start.26
  149.7 1.3 collective-permute-start.25
  151.0 6.9 %collective-permute-start.24 = (f32[8,1]{1,0:T(8,128)S(1)}, f32[8,1]{1,0:T(8,128)S(1)}, u32[]{:S(2)}, u32[]{:S(2)}) collective-permute-start(f32[8,1]{1,0:T(8,128)S(1)} %get-tuple-element.11), channel_id=1, source_target_pairs={{0,2},{2,4},{4,6},{6,8},{8,10},{10,12},{12,14},{14,16},{16,18},{18... | collective-permute-start | bytes 104 | tf_op jit(solution)/shard_map/ppermute | solution.py:27
  157.9 1.3 collective-permute-done.24
  159.2 0.7 fusion.38
  159.9 1.9 collective-permute-start.29
  161.8 2.4 collective-permute-start.33
  164.3 1.3 collective-permute-start.28
  165.6 6.9 %collective-permute-start.27 = (f32[8,1]{1,0:T(8,128)S(1)}, f32[8,1]{1,0:T(8,128)S(1)}, u32[]{:S(2)}, u32[]{:S(2)}) collective-permute-start(f32[8,1]{1,0:T(8,128)S(1)} %get-tuple-element.9), channel_id=1, source_target_pairs={{0,2},{2,4},{4,6},{6,8},{8,10},{10,12},{12,14},{14,16},{16,18},{18... | collective-permute-start | bytes 104 | tf_op jit(solution)/shard_map/ppermute | solution.py:27
  173.1 0.7 collective-permute-done.27
  174.3 1.9 collective-permute-start.32
  176.3 1.3 collective-permute-start.31
  177.6 6.9 %collective-permute-start.30 = (f32[8,1]{1,0:T(8,128)S(1)}, f32[8,1]{1,0:T(8,128)S(1)}, u32[]{:S(2)}, u32[]{:S(2)}) collective-permute-start(f32[8,1]{1,0:T(8,128)S(1)} %get-tuple-element.7), channel_id=1, source_target_pairs={{0,2},{2,4},{4,6},{6,8},{8,10},{10,12},{12,14},{14,16},{16,18},{18... | collective-permute-start | bytes 104 | tf_op jit(solution)/shard_map/ppermute | solution.py:27
  185.1 0.7 collective-permute-done.30
  186.2 2.1 scatter_custom_fusion.1
  188.3 240.1 %reduce-scatter.2.cloned.1.call-done = f32[64,128]{1,0:T(8,128)} async-done(((f32[2048,128]{1,0:T(8,128)}), f32[64,128]{1,0:T(8,128)}) %reduce-scatter.2.cloned.1.call-update) | async-done | bytes 32784 | tf_op jit(solution)/shard_map/reduce_scatter | solution.py:86
  428.4 46.9 %psum.7 = f32[64,128]{1,0:T(8,128)} all-reduce(f32[64,128]{1,0:T(8,128)} %reduce-scatter.2.cloned.1.call-done), channel_id=1, replica_groups=mesh['group'=8,'mesh'=32,'comp'=2] {'group','comp'}, use_global_device_ids=true, to_apply=%region_4.5 | all-reduce | flops 8192 | bytes 65536 | tf_op jit(solution)/shard_map/psum | solution.py:94
  (66 shorter events, 7.2 us)
Async XLA Ops:
  6.5 23.0 %copy-start = (f32[128,128]{1,0:T(8,128)S(1)}, f32[128,128]{1,0:T(8,128)}, u32[]{:S(2)}) copy-start(f32[128,128]{1,0:T(8,128)} %param.10) | copy-start | bytes 196612
  6.5 54.8 %copy-start.1 = (f32[1,1,8,128,128]{4,3,2,1,0:T(8,128)S(1)}, f32[1,1,8,128,128]{4,3,2,1,0:T(8,128)}, u32[]{:S(2)}) copy-start(f32[1,1,8,128,128]{4,3,2,1,0:T(8,128)} %param.11) | copy-start | bytes 1572868
  8.5 41.2 %all-to-all-start = ((f32[32,64,128]{2,1,0:T(8,128)}), f32[32,64,128]{2,1,0:T(8,128)S(1)}, u32[]{:S(2)}, u32[]{:S(2)}) async-start(f32[32,64,128]{2,1,0:T(8,128)} %stack.2), calls=%async_computation | async-start | bytes 2097152 | tf_op jit(solution)/shard_map/all_to_all | solution.py:68
  21.6 406.8 %reduce-scatter.2.cloned.1.call-start = ((), (), s32[]{:S(2)}) async-start(), calls=%async_computation.2 | async-start | bytes 1081344 | tf_op jit(solution)/shard_map/reduce_scatter | solution.py:86
  21.7 28.8 %collective-permute-start.1 = (f32[8,1]{1,0:T(8,128)S(1)}, f32[8,1]{1,0:T(8,128)S(1)}, u32[]{:S(2)}, u32[]{:S(2)}) collective-permute-start(f32[8,1]{1,0:T(8,128)S(1)} %broadcast.159), channel_id=1, source_target_pairs={{2,0},{4,2},{6,4},{8,6},{10,8},{12,10},{14,12},{16,14},{18,16},{20... | collective-permute-start | bytes 104 | tf_op jit(solution)/shard_map/ppermute | solution.py:28
  23.0 27.5 %collective-permute-start = (f32[8,1]{1,0:T(8,128)S(1)}, f32[8,1]{1,0:T(8,128)S(1)}, u32[]{:S(2)}, u32[]{:S(2)}) collective-permute-start(f32[8,1]{1,0:T(8,128)S(1)} %broadcast.159), channel_id=1, source_target_pairs={{0,2},{2,4},{4,6},{6,8},{8,10},{10,12},{12,14},{14,16},{16,18},{18... | collective-permute-start | bytes 104 | tf_op jit(solution)/shard_map/ppermute | solution.py:27
  27.6 66.7 %copy-start.3 = (s32[1,128]{1,0:T(1,128)S(1)}, s32[1,128]{1,0:T(1,128)}, u32[]{:S(2)}) copy-start(s32[1,128]{1,0:T(1,128)} %param.12) | copy-start | bytes 1540
  27.6 66.7 %copy-start.2 = (f32[1,1,8,128]{3,2,1,0:T(8,128)S(1)}, f32[1,1,8,128]{3,2,1,0:T(8,128)}, u32[]{:S(2)}) copy-start(f32[1,1,8,128]{3,2,1,0:T(8,128)} %param.13) | copy-start | bytes 12292
  27.6 22.9 %collective-permute-start.2 = (f32[8,16384]{1,0:T(8,128)S(1)}, f32[8,16384]{1,0:T(8,128)S(1)}, u32[]{:S(2)}, u32[]{:S(2)}) collective-permute-start(f32[8,16384]{1,0:T(8,128)S(1)} %broadcast.156.clone), channel_id=1, source_target_pairs={{0,1},{1,0},{2,3},{3,2},{4,5},{5,4},{6,7},{7,6},{8,9},{9,8},{10,11... | collective-permute-start | bytes 1572872 | tf_op jit(solution)/shard_map/ppermute | solution.py:17
  52.1 9.2 %collective-permute-start.5 = (f32[8,16384]{1,0:T(8,128)S(1)}, f32[8,16384]{1,0:T(8,128)S(1)}, u32[]{:S(2)}, u32[]{:S(2)}) collective-permute-start(f32[8,16384]{1,0:T(8,128)S(1)} %fusion.8), channel_id=1, source_target_pairs={{0,1},{1,0},{2,3},{3,2},{4,5},{5,4},{6,7},{7,6},{8,9},{9,8},{10,11... | collective-permute-start | bytes 1572872 | tf_op jit(solution)/shard_map/ppermute | solution.py:17
  54.1 5.8 %collective-permute-start.4 = (f32[8,1]{1,0:T(8,128)S(1)}, f32[8,1]{1,0:T(8,128)S(1)}, u32[]{:S(2)}, u32[]{:S(2)}) collective-permute-start(f32[8,1]{1,0:T(8,128)S(1)} %get-tuple-element.26), channel_id=1, source_target_pairs={{2,0},{4,2},{6,4},{8,6},{10,8},{12,10},{14,12},{16,14},{18,16},{20... | collective-permute-start | bytes 104 | tf_op jit(solution)/shard_map/ppermute | solution.py:28
  55.4 5.9 %collective-permute-start.3 = (f32[8,1]{1,0:T(8,128)S(1)}, f32[8,1]{1,0:T(8,128)S(1)}, u32[]{:S(2)}, u32[]{:S(2)}) collective-permute-start(f32[8,1]{1,0:T(8,128)S(1)} %get-tuple-element.25), channel_id=1, source_target_pairs={{0,2},{2,4},{4,6},{6,8},{8,10},{10,12},{12,14},{14,16},{16,18},{18... | collective-permute-start | bytes 104 | tf_op jit(solution)/shard_map/ppermute | solution.py:27
  62.2 9.4 %collective-permute-start.8 = (f32[8,16384]{1,0:T(8,128)S(1)}, f32[8,16384]{1,0:T(8,128)S(1)}, u32[]{:S(2)}, u32[]{:S(2)}) collective-permute-start(f32[8,16384]{1,0:T(8,128)S(1)} %fusion.10), channel_id=1, source_target_pairs={{0,1},{1,0},{2,3},{3,2},{4,5},{5,4},{6,7},{7,6},{8,9},{9,8},{10,11... | collective-permute-start | bytes 1572872 | tf_op jit(solution)/shard_map/ppermute | solution.py:17
  64.2 6.7 %collective-permute-start.7 = (f32[8,1]{1,0:T(8,128)S(1)}, f32[8,1]{1,0:T(8,128)S(1)}, u32[]{:S(2)}, u32[]{:S(2)}) collective-permute-start(f32[8,1]{1,0:T(8,128)S(1)} %get-tuple-element.24), channel_id=1, source_target_pairs={{2,0},{4,2},{6,4},{8,6},{10,8},{12,10},{14,12},{16,14},{18,16},{20... | collective-permute-start | bytes 104 | tf_op jit(solution)/shard_map/ppermute | solution.py:28
  65.5 6.1 %collective-permute-start.6 = (f32[8,1]{1,0:T(8,128)S(1)}, f32[8,1]{1,0:T(8,128)S(1)}, u32[]{:S(2)}, u32[]{:S(2)}) collective-permute-start(f32[8,1]{1,0:T(8,128)S(1)} %get-tuple-element.23), channel_id=1, source_target_pairs={{0,2},{2,4},{4,6},{6,8},{8,10},{10,12},{12,14},{14,16},{16,18},{18... | collective-permute-start | bytes 104 | tf_op jit(solution)/shard_map/ppermute | solution.py:27
  72.1 9.4 %collective-permute-start.11 = (f32[8,16384]{1,0:T(8,128)S(1)}, f32[8,16384]{1,0:T(8,128)S(1)}, u32[]{:S(2)}, u32[]{:S(2)}) collective-permute-start(f32[8,16384]{1,0:T(8,128)S(1)} %fusion.12), channel_id=1, source_target_pairs={{0,1},{1,0},{2,3},{3,2},{4,5},{5,4},{6,7},{7,6},{8,9},{9,8},{10,11... | collective-permute-start | bytes 1572872 | tf_op jit(solution)/shard_map/ppermute | solution.py:17
  74.1 6.1 %collective-permute-start.10 = (f32[8,1]{1,0:T(8,128)S(1)}, f32[8,1]{1,0:T(8,128)S(1)}, u32[]{:S(2)}, u32[]{:S(2)}) collective-permute-start(f32[8,1]{1,0:T(8,128)S(1)} %get-tuple-element.22), channel_id=1, source_target_pairs={{2,0},{4,2},{6,4},{8,6},{10,8},{12,10},{14,12},{16,14},{18,16},{20... | collective-permute-start | bytes 104 | tf_op jit(solution)/shard_map/ppermute | solution.py:28
  75.4 6.1 %collective-permute-start.9 = (f32[8,1]{1,0:T(8,128)S(1)}, f32[8,1]{1,0:T(8,128)S(1)}, u32[]{:S(2)}, u32[]{:S(2)}) collective-permute-start(f32[8,1]{1,0:T(8,128)S(1)} %get-tuple-element.21), channel_id=1, source_target_pairs={{0,2},{2,4},{4,6},{6,8},{8,10},{10,12},{12,14},{14,16},{16,18},{18... | collective-permute-start | bytes 104 | tf_op jit(solution)/shard_map/ppermute | solution.py:27
  82.5 9.4 %collective-permute-start.14 = (f32[8,16384]{1,0:T(8,128)S(1)}, f32[8,16384]{1,0:T(8,128)S(1)}, u32[]{:S(2)}, u32[]{:S(2)}) collective-permute-start(f32[8,16384]{1,0:T(8,128)S(1)} %fusion.14), channel_id=1, source_target_pairs={{0,1},{1,0},{2,3},{3,2},{4,5},{5,4},{6,7},{7,6},{8,9},{9,8},{10,11... | collective-permute-start | bytes 1572872 | tf_op jit(solution)/shard_map/ppermute | solution.py:17
  84.5 6.7 %collective-permute-start.13 = (f32[8,1]{1,0:T(8,128)S(1)}, f32[8,1]{1,0:T(8,128)S(1)}, u32[]{:S(2)}, u32[]{:S(2)}) collective-permute-start(f32[8,1]{1,0:T(8,128)S(1)} %get-tuple-element.20), channel_id=1, source_target_pairs={{2,0},{4,2},{6,4},{8,6},{10,8},{12,10},{14,12},{16,14},{18,16},{20... | collective-permute-start | bytes 104 | tf_op jit(solution)/shard_map/ppermute | solution.py:28
  85.7 6.1 %collective-permute-start.12 = (f32[8,1]{1,0:T(8,128)S(1)}, f32[8,1]{1,0:T(8,128)S(1)}, u32[]{:S(2)}, u32[]{:S(2)}) collective-permute-start(f32[8,1]{1,0:T(8,128)S(1)} %get-tuple-element.19), channel_id=1, source_target_pairs={{0,2},{2,4},{4,6},{6,8},{8,10},{10,12},{12,14},{14,16},{16,18},{18... | collective-permute-start | bytes 104 | tf_op jit(solution)/shard_map/ppermute | solution.py:27
  92.4 12.0 %collective-permute-start.17 = (f32[8,16384]{1,0:T(8,128)S(1)}, f32[8,16384]{1,0:T(8,128)}, u32[]{:S(2)}, u32[]{:S(2)}) collective-permute-start(f32[8,16384]{1,0:T(8,128)S(1)} %fusion.16), channel_id=1, source_target_pairs={{0,1},{1,0},{2,3},{3,2},{4,5},{5,4},{6,7},{7,6},{8,9},{9,8},{10,11... | collective-permute-start | bytes 1572872 | tf_op jit(solution)/shard_map/ppermute | solution.py:17
  95.1 8.0 %collective-permute-start.16 = (f32[8,1]{1,0:T(8,128)S(1)}, f32[8,1]{1,0:T(8,128)S(1)}, u32[]{:S(2)}, u32[]{:S(2)}) collective-permute-start(f32[8,1]{1,0:T(8,128)S(1)} %get-tuple-element.18), channel_id=1, source_target_pairs={{2,0},{4,2},{6,4},{8,6},{10,8},{12,10},{14,12},{16,14},{18,16},{20... | collective-permute-start | bytes 104 | tf_op jit(solution)/shard_map/ppermute | solution.py:28
  96.4 8.0 %collective-permute-start.15 = (f32[8,1]{1,0:T(8,128)S(1)}, f32[8,1]{1,0:T(8,128)S(1)}, u32[]{:S(2)}, u32[]{:S(2)}) collective-permute-start(f32[8,1]{1,0:T(8,128)S(1)} %get-tuple-element.17), channel_id=1, source_target_pairs={{0,2},{2,4},{4,6},{6,8},{8,10},{10,12},{12,14},{14,16},{16,18},{18... | collective-permute-start | bytes 104 | tf_op jit(solution)/shard_map/ppermute | solution.py:27
  123.6 11.5 %collective-permute-start.20 = (f32[8,16384]{1,0:T(8,128)S(1)}, f32[8,16384]{1,0:T(8,128)S(1)}, u32[]{:S(2)}, u32[]{:S(2)}) collective-permute-start(f32[8,16384]{1,0:T(8,128)S(1)} %fusion.5), channel_id=1, source_target_pairs={{0,1},{1,0},{2,3},{3,2},{4,5},{5,4},{6,7},{7,6},{8,9},{9,8},{10,11... | collective-permute-start | bytes 1572872 | tf_op jit(solution)/shard_map/ppermute | solution.py:17
  125.6 8.2 %collective-permute-start.19 = (f32[8,1]{1,0:T(8,128)S(1)}, f32[8,1]{1,0:T(8,128)S(1)}, u32[]{:S(2)}, u32[]{:S(2)}) collective-permute-start(f32[8,1]{1,0:T(8,128)S(1)} %get-tuple-element.16), channel_id=1, source_target_pairs={{2,0},{4,2},{6,4},{8,6},{10,8},{12,10},{14,12},{16,14},{18,16},{20... | collective-permute-start | bytes 104 | tf_op jit(solution)/shard_map/ppermute | solution.py:28
  126.8 8.2 %collective-permute-start.18 = (f32[8,1]{1,0:T(8,128)S(1)}, f32[8,1]{1,0:T(8,128)S(1)}, u32[]{:S(2)}, u32[]{:S(2)}) collective-permute-start(f32[8,1]{1,0:T(8,128)S(1)} %get-tuple-element.15), channel_id=1, source_target_pairs={{0,2},{2,4},{4,6},{6,8},{8,10},{10,12},{12,14},{14,16},{16,18},{18... | collective-permute-start | bytes 104 | tf_op jit(solution)/shard_map/ppermute | solution.py:27
  135.7 11.6 %collective-permute-start.23 = (f32[8,16384]{1,0:T(8,128)S(1)}, f32[8,16384]{1,0:T(8,128)S(1)}, u32[]{:S(2)}, u32[]{:S(2)}) collective-permute-start(f32[8,16384]{1,0:T(8,128)S(1)} %fusion.50), channel_id=1, source_target_pairs={{0,1},{1,0},{2,3},{3,2},{4,5},{5,4},{6,7},{7,6},{8,9},{9,8},{10,11... | collective-permute-start | bytes 1572872 | tf_op jit(solution)/shard_map/ppermute | solution.py:17
  137.7 8.8 %collective-permute-start.22 = (f32[8,1]{1,0:T(8,128)S(1)}, f32[8,1]{1,0:T(8,128)S(1)}, u32[]{:S(2)}, u32[]{:S(2)}) collective-permute-start(f32[8,1]{1,0:T(8,128)S(1)} %get-tuple-element.14), channel_id=1, source_target_pairs={{2,0},{4,2},{6,4},{8,6},{10,8},{12,10},{14,12},{16,14},{18,16},{20... | collective-permute-start | bytes 104 | tf_op jit(solution)/shard_map/ppermute | solution.py:28
  139.0 8.3 %collective-permute-start.21 = (f32[8,1]{1,0:T(8,128)S(1)}, f32[8,1]{1,0:T(8,128)S(1)}, u32[]{:S(2)}, u32[]{:S(2)}) collective-permute-start(f32[8,1]{1,0:T(8,128)S(1)} %get-tuple-element.13), channel_id=1, source_target_pairs={{0,2},{2,4},{4,6},{6,8},{8,10},{10,12},{12,14},{14,16},{16,18},{18... | collective-permute-start | bytes 104 | tf_op jit(solution)/shard_map/ppermute | solution.py:27
  147.7 11.5 %collective-permute-start.26 = (f32[8,16384]{1,0:T(8,128)S(1)}, f32[8,16384]{1,0:T(8,128)S(1)}, u32[]{:S(2)}, u32[]{:S(2)}) collective-permute-start(f32[8,16384]{1,0:T(8,128)S(1)} %fusion.44), channel_id=1, source_target_pairs={{0,1},{1,0},{2,3},{3,2},{4,5},{5,4},{6,7},{7,6},{8,9},{9,8},{10,11... | collective-permute-start | bytes 1572872 | tf_op jit(solution)/shard_map/ppermute | solution.py:17
  149.7 8.2 %collective-permute-start.25 = (f32[8,1]{1,0:T(8,128)S(1)}, f32[8,1]{1,0:T(8,128)S(1)}, u32[]{:S(2)}, u32[]{:S(2)}) collective-permute-start(f32[8,1]{1,0:T(8,128)S(1)} %get-tuple-element.12), channel_id=1, source_target_pairs={{2,0},{4,2},{6,4},{8,6},{10,8},{12,10},{14,12},{16,14},{18,16},{20... | collective-permute-start | bytes 104 | tf_op jit(solution)/shard_map/ppermute | solution.py:28
  151.0 8.2 %collective-permute-start.24 = (f32[8,1]{1,0:T(8,128)S(1)}, f32[8,1]{1,0:T(8,128)S(1)}, u32[]{:S(2)}, u32[]{:S(2)}) collective-permute-start(f32[8,1]{1,0:T(8,128)S(1)} %get-tuple-element.11), channel_id=1, source_target_pairs={{0,2},{2,4},{4,6},{6,8},{8,10},{10,12},{12,14},{14,16},{16,18},{18... | collective-permute-start | bytes 104 | tf_op jit(solution)/shard_map/ppermute | solution.py:27
  159.9 14.0 %collective-permute-start.29 = (f32[8,16384]{1,0:T(8,128)S(1)}, f32[8,16384]{1,0:T(8,128)S(1)}, u32[]{:S(2)}, u32[]{:S(2)}) collective-permute-start(f32[8,16384]{1,0:T(8,128)S(1)} %fusion.38), channel_id=1, source_target_pairs={{0,1},{1,0},{2,3},{3,2},{4,5},{5,4},{6,7},{7,6},{8,9},{9,8},{10,11... | collective-permute-start | bytes 1572872 | tf_op jit(solution)/shard_map/ppermute | solution.py:17
  161.8 23.2 %collective-permute-start.33 = (f32[8,16384]{1,0:T(8,128)S(1)}, f32[8,16384]{1,0:T(8,128)S(1)}, u32[]{:S(2)}, u32[]{:S(2)}) collective-permute-start(f32[8,16384]{1,0:T(8,128)S(1)} %fusion.18), channel_id=1, source_target_pairs={{0,1},{1,0},{2,3},{3,2},{4,5},{5,4},{6,7},{7,6},{8,9},{9,8},{10,11... | collective-permute-start | bytes 1572872 | tf_op jit(solution)/shard_map/ppermute | solution.py:17
  164.3 8.8 %collective-permute-start.28 = (f32[8,1]{1,0:T(8,128)S(1)}, f32[8,1]{1,0:T(8,128)S(1)}, u32[]{:S(2)}, u32[]{:S(2)}) collective-permute-start(f32[8,1]{1,0:T(8,128)S(1)} %get-tuple-element.10), channel_id=1, source_target_pairs={{2,0},{4,2},{6,4},{8,6},{10,8},{12,10},{14,12},{16,14},{18,16},{20... | collective-permute-start | bytes 104 | tf_op jit(solution)/shard_map/ppermute | solution.py:28
  165.6 8.2 %collective-permute-start.27 = (f32[8,1]{1,0:T(8,128)S(1)}, f32[8,1]{1,0:T(8,128)S(1)}, u32[]{:S(2)}, u32[]{:S(2)}) collective-permute-start(f32[8,1]{1,0:T(8,128)S(1)} %get-tuple-element.9), channel_id=1, source_target_pairs={{0,2},{2,4},{4,6},{6,8},{8,10},{10,12},{12,14},{14,16},{16,18},{18... | collective-permute-start | bytes 104 | tf_op jit(solution)/shard_map/ppermute | solution.py:27
  174.3 11.5 %collective-permute-start.32 = (f32[8,16384]{1,0:T(8,128)S(1)}, f32[8,16384]{1,0:T(8,128)S(1)}, u32[]{:S(2)}, u32[]{:S(2)}) collective-permute-start(f32[8,16384]{1,0:T(8,128)S(1)} %fusion.32), channel_id=1, source_target_pairs={{0,1},{1,0},{2,3},{3,2},{4,5},{5,4},{6,7},{7,6},{8,9},{9,8},{10,11... | collective-permute-start | bytes 1572872 | tf_op jit(solution)/shard_map/ppermute | solution.py:17
  176.3 8.8 %collective-permute-start.31 = (f32[8,1]{1,0:T(8,128)S(1)}, f32[8,1]{1,0:T(8,128)S(1)}, u32[]{:S(2)}, u32[]{:S(2)}) collective-permute-start(f32[8,1]{1,0:T(8,128)S(1)} %get-tuple-element.8), channel_id=1, source_target_pairs={{2,0},{4,2},{6,4},{8,6},{10,8},{12,10},{14,12},{16,14},{18,16},{20... | collective-permute-start | bytes 104 | tf_op jit(solution)/shard_map/ppermute | solution.py:28
  177.6 8.2 %collective-permute-start.30 = (f32[8,1]{1,0:T(8,128)S(1)}, f32[8,1]{1,0:T(8,128)S(1)}, u32[]{:S(2)}, u32[]{:S(2)}) collective-permute-start(f32[8,1]{1,0:T(8,128)S(1)} %get-tuple-element.7), channel_id=1, source_target_pairs={{0,2},{2,4},{4,6},{6,8},{8,10},{10,12},{12,14},{14,16},{16,18},{18... | collective-permute-start | bytes 104 | tf_op jit(solution)/shard_map/ppermute | solution.py:27
Sparse Core Ops, SparseCore 0:
  188.5 239.9 reduce-scatter.1
